TPU v7x, 256 devices: a whole 4x4x8 slice. The times are simulated.
256 devices in a mesh: segment: 8 (over y, z_lo), frame: 32 (over x, z_hi, core).
Axes of the slice: x: 4, y: 4, z: 8 (z_hi: 4, z_lo: 2; z = z_hi * 2 + z_lo), core: 2. Of those that a mesh axis runs over, the one named last changes fastest.
Arguments:
- noisy_clips: bfloat16 [4, 32, 16, 16, 512], P(None, 'frame'), may hold values from -6 to 6
- conv_first: bfloat16 [8, 9, 512, 512], P('segment', None, 'frame'), may hold values from -0.09375 to 0.09375
- conv_second: bfloat16 [8, 9, 512, 512], P('segment', None, 'frame'), may hold values from -0.09375 to 0.09375
- temporal: bfloat16 [8, 3, 512, 512], P('segment', None, 'frame'), may hold values from -0.15625 to 0.15625
Outputs:
- denoised: bfloat16 [4, 32, 16, 16, 512], P(None, 'frame', 'segment')
All inputs are finite; a program needn't handle non-finite values.
Results may differ from a plain program's by a relative error of at most 0.013.
Values may be sent and summed in bfloat16 or wider, within the bound.
No kernel may reach another device: no remote copies, remote signals or barrier semaphores. Data moves between devices by JAX's collectives and lax.ppermute only.
A program may use at most 64 MiB of HBM per device.

v0:
```python
import jax
import jax.numpy as jnp
from jax import lax
from jax.sharding import PartitionSpec as P

skip_scale = 0.7071067811865476


def passed_along(shard, axis, by):
    length = lax.axis_size(axis)
    pairs = [(i, i + by) for i in range(length) if 0 <= i + by < length]
    return lax.ppermute(shard, axis, pairs)


def partner(shard, axis, bit):
    return lax.ppermute(shard, axis, [(i, i ^ 1 << bit) for i in range(lax.axis_size(axis))])


def extended_2(cells, sides, width):
    for axis, dim in sides:
        count = lax.axis_size(axis)
        ends = count - 1
        head = lax.slice_in_dim(cells, 0, width, axis=dim)
        tail = lax.slice_in_dim(cells, cells.shape[dim] - width, cells.shape[dim], axis=dim)
        cells = jnp.concatenate(
            [
                lax.ppermute(tail, axis, [(i, (i + 1) % count) for i in range(ends)]),
                cells,
                lax.ppermute(head, axis, [((i + 1) % count, i) for i in range(ends)]),
            ],
            axis=dim,
        )
    return cells


def broadcast(shard, axis, root):
    mine = lax.axis_index(axis) == root
    return lax.psum(jnp.where(mine, shard, jnp.zeros_like(shard)), axis)


def spatial(field_in, kernel):
    extent = field_in.shape[1]
    channels = field_in.shape[3]
    padded = jnp.pad(field_in, ((0, 0), (1, 1), (1, 1), (0, 0)))
    accumulated = jnp.zeros((field_in.shape[0] * extent * extent, channels), jnp.float32)
    for row_shift in range(3):
        for col_shift in range(3):
            window = padded[
                :, row_shift : row_shift + extent, col_shift : col_shift + extent, :
            ].reshape(-1, channels)
            accumulated = accumulated + jnp.dot(
                window, kernel[3 * row_shift + col_shift], preferred_element_type=jnp.float32
            )
    return accumulated.reshape(field_in.shape)


def temporal_mix(extended, kernel, frame_local):
    channels = extended.shape[3]
    out_shape = (frame_local,) + extended.shape[1:]
    accumulated = jnp.zeros(out_shape, jnp.float32)
    for offset in range(3):
        window = extended[offset : offset + frame_local].reshape(-1, channels)
        accumulated = accumulated + jnp.dot(
            window, kernel[offset], preferred_element_type=jnp.float32
        ).reshape(out_shape)
    return accumulated


def on_device(noisy_clips, conv_first, conv_second, temporal):
    sections = lax.axis_size("segment")
    segment_id = lax.axis_index("segment")
    first_full, second_full, time_full = (
        lax.all_gather(conv_first, "frame", axis=2, tiled=True),
        lax.all_gather(conv_second, "frame", axis=2, tiled=True),
        lax.all_gather(temporal, "frame", axis=2, tiled=True),
    )
    first_kernel = first_full[0]
    second_kernel = second_full[0]
    time_kernel = time_full[0]
    clip_count = noisy_clips.shape[0]
    frame_local = noisy_clips.shape[1]
    side_len = noisy_clips.shape[2]
    block_shape = noisy_clips.shape[1:]
    tick_count = clip_count + sections - 1
    half_sections = sections // 2
    is_up = segment_id >= half_sections
    side_store = jnp.zeros((clip_count,) + block_shape, jnp.bfloat16)
    out_store = jnp.zeros(noisy_clips.shape, jnp.bfloat16)
    prev_out = jnp.zeros(block_shape, jnp.bfloat16)

    def tick_step(carry, tick_index):
        prev_out, side_store, out_store = carry
        clip_now = tick_index - segment_id
        active = (clip_now >= 0) & (clip_now < clip_count)
        clip_slot = jnp.clip(clip_now, 0, clip_count - 1)
        own_input = lax.dynamic_index_in_dim(noisy_clips, clip_slot, 0, keepdims=False)
        received = passed_along(prev_out, "segment", 1)
        entering = jnp.where(segment_id == 0, own_input, received)
        mirrored = entering
        for bit_number in range(sections.bit_length() - 1):
            mirrored = partner(mirrored, "segment", bit_number)
        mirror_clip = tick_index - (sections - 1 - segment_id)
        written = (jnp.arange(clip_count) == mirror_clip) & is_up
        side_store = jnp.where(written[:, None, None, None, None], mirrored[None], side_store)
        skip_feature = lax.dynamic_index_in_dim(side_store, clip_slot, 0, keepdims=False)
        joined = (
            (entering.astype(jnp.float32) + skip_feature.astype(jnp.float32)) * skip_scale
        ).astype(jnp.bfloat16)
        section_in = jnp.where(is_up, joined, entering)
        activated = lax.cond(
            active,
            lambda: jax.nn.silu(spatial(section_in, first_kernel)).astype(jnp.bfloat16),
            lambda: jnp.zeros(block_shape, jnp.bfloat16),
        )
        extended = extended_2(activated, (("frame", 0),), 1)

        def second_pass():
            branch_sum = spatial(activated, second_kernel) + temporal_mix(
                extended, time_kernel, frame_local
            )
            return (section_in.astype(jnp.float32) + jax.nn.silu(branch_sum)).astype(jnp.bfloat16)

        section_out = lax.cond(active, second_pass, lambda: jnp.zeros(block_shape, jnp.bfloat16))
        finished = (jnp.arange(clip_count) == clip_slot) & active & (segment_id == sections - 1)
        out_store = jnp.where(finished[:, None, None, None, None], section_out[None], out_store)
        return ((section_out, side_store, out_store), None)

    final_carry, unused = lax.scan(
        tick_step, (prev_out, side_store, out_store), jnp.arange(tick_count, dtype=jnp.int32)
    )
    delivered = broadcast(final_carry[2], "segment", sections - 1)
    slab_rows = side_len // sections
    return lax.dynamic_slice_in_dim(delivered, segment_id * slab_rows, slab_rows, 2)


def solution(mesh):
    in_specs = (
        P(None, "frame", None, None, None),
        P("segment", None, "frame", None),
        P("segment", None, "frame", None),
        P("segment", None, "frame", None),
    )
    out_specs = P(None, "frame", "segment", None, None)
    return jax.shard_map(
        on_device, mesh=mesh, in_specs=in_specs, out_specs=out_specs, check_vma=False
    )
```

profile of v0, /device:TPU:2, one launch (start us, length us, event | category | flops | bytes accessed | tf_op | source)
XLA Modules:
  0.0 975.8 jit_solution(13421447813197799213)
XLA Ops:
  8.8 56.3 %all-gather.8.cloned.1.call-done = bf16[1,3,512,512]{3,2,1,0:T(8,128)(2,1)} async-done(((bf16[1,3,16,512]{3,2,1,0:T(8,128)(2,1)}), bf16[1,3,512,512]{3,2,1,0:T(8,128)(2,1)}) %all-gather.8.cloned.1.call-update) | async-done | bytes 1572880 | tf_op jit(solution)/shard_map/all_gather | solution.py:75
  65.1 63.4 %all-gather.4.cloned.1.call-done = bf16[1,9,512,512]{3,2,1,0:T(8,128)(2,1)} async-done(((bf16[1,9,16,512]{3,2,1,0:T(8,128)(2,1)}), bf16[1,9,512,512]{3,2,1,0:T(8,128)(2,1)}) %all-gather.4.cloned.1.call-update) | async-done | bytes 4718608 | tf_op jit(solution)/shard_map/all_gather | solution.py:73
  128.4 63.1 %all-gather.6.cloned.1.call-done = bf16[1,9,512,512]{3,2,1,0:T(8,128)(2,1)} async-done(((bf16[1,9,16,512]{3,2,1,0:T(8,128)(2,1)}), bf16[1,9,512,512]{3,2,1,0:T(8,128)(2,1)}) %all-gather.6.cloned.1.call-update) | async-done | bytes 4718608 | tf_op jit(solution)/shard_map/all_gather | solution.py:74
  192.3 682.3 %while.16 = (s32[]{:T(128)}, bf16[1,16,16,512]{3,2,1,0:T(8,128)(2,1)}, bf16[4,1,16,16,512]{4,3,2,1,0:T(8,128)(2,1)S(1)}, bf16[4,1,16,16,512]{4,3,2,1,0:T(8,128)(...) while((s32[]{:T(128)}, ...), condition=%wide.region_5.6_spmd.clone, body=%wide.region_0.5_spmd.clone.sunk | while | flops 2825650176 | bytes 99615424 | solution.py:128
  234.9 6.7 collective-permute-start.5
  245.5 7.0 conditional.7
  270.5 7.6 collective-permute-done.2
  278.8 7.2 collective-permute-done.3
  293.9 6.7 collective-permute-start.5
  307.3 7.0 conditional.7
  342.1 7.3 collective-permute-done.3
  357.3 6.7 collective-permute-start.5
  370.6 7.0 conditional.7
  397.8 7.7 collective-permute-done.2
  406.1 7.2 collective-permute-done.3
  421.2 6.7 collective-permute-start.5
  434.5 7.0 conditional.7
  468.4 7.5 collective-permute-done.3
  478.5 6.7 collective-permute-start.5
  491.1 14.6 %collective-permute-start = (bf16[1,16,16,512]{3,2,1,0:T(8,128)(2,1)}, bf16[1,16,16,512]{3,2,1,0:T(8,128)(2,1)S(1)}, u32[]{:S(2)}, u32[]{:S(2)}) collective-permute-start(bf16[1,16,16,512]{3,2,1,0:T(8,128)(2,1)} %get-tuple-element.343), channel_id=1, source_target_pairs={{0,32},{32,64},{64,96},{96,128},{128,160},{160,192},{192,224},{1,3... | collective-permute-start | bytes 786440 | tf_op jit(solution)/shard_map/while/body/eval_jaxpr/ppermute | solution.py:12
  510.8 6.9 collective-permute-start.1
  531.0 7.2 collective-permute-done.3
  562.9 15.2 %collective-permute-start.1 = (bf16[1,16,16,512]{3,2,1,0:T(8,128)(2,1)S(1)}, bf16[1,16,16,512]{3,2,1,0:T(8,128)(2,1)S(1)}, u32[]{:S(2)}, u32[]{:S(2)}) collective-permute-start(bf16[1,16,16,512]{3,2,1,0:T(8,128)(2,1)S(1)} %bitcast_select_fusion.2), channel_id=1, source_target_pairs={{0,32},{32,0},{64,96},{96,64},{128,160},{160,128},{192,224},{224,1... | collective-permute-start | bytes 786440 | tf_op jit(solution)/shard_map/while/body/eval_jaxpr/ppermute | solution.py:16
  594.0 7.3 collective-permute-done.3
  603.8 6.7 collective-permute-start.5
  637.9 11.0 %collective-permute-start.2 = (bf16[1,16,16,512]{3,2,1,0:T(8,128)(2,1)S(1)}, bf16[1,16,16,512]{3,2,1,0:T(8,128)(2,1)S(1)}, u32[]{:S(2)}, u32[]{:S(2)}) collective-permute-start(bf16[1,16,16,512]{3,2,1,0:T(8,128)(2,1)S(1)} %collective-permute-done.1), channel_id=1, source_target_pairs={{0,64},{32,96},{64,0},{96,32},{128,192},{160,224},{192,128},{224,1... | collective-permute-start | bytes 786440 | tf_op jit(solution)/shard_map/while/body/eval_jaxpr/ppermute | solution.py:16
  666.8 6.7 collective-permute-start.5
  699.2 13.0 %collective-permute-start.2 = (bf16[1,16,16,512]{3,2,1,0:T(8,128)(2,1)S(1)}, bf16[1,16,16,512]{3,2,1,0:T(8,128)(2,1)S(1)}, u32[]{:S(2)}, u32[]{:S(2)}) collective-permute-start(bf16[1,16,16,512]{3,2,1,0:T(8,128)(2,1)S(1)} %collective-permute-done.1), channel_id=1, source_target_pairs={{0,64},{32,96},{64,0},{96,32},{128,192},{160,224},{192,128},{224,1... | collective-permute-start | bytes 786440 | tf_op jit(solution)/shard_map/while/body/eval_jaxpr/ppermute | solution.py:16
  767.6 19.2 %collective-permute-start.3 = (bf16[1,16,16,512]{3,2,1,0:T(8,128)(2,1)S(1)}, bf16[1,16,16,512]{3,2,1,0:T(8,128)(2,1)S(1)}, u32[]{:S(2)}, u32[]{:S(2)}) collective-permute-start(bf16[1,16,16,512]{3,2,1,0:T(8,128)(2,1)S(1)} %collective-permute-done.2), channel_id=1, source_target_pairs={{0,128},{32,160},{64,192},{96,224},{128,0},{160,32},{192,64},{224,... | collective-permute-start | bytes 786440 | tf_op jit(solution)/shard_map/while/body/eval_jaxpr/ppermute | solution.py:16
  793.6 6.7 collective-permute-start.5
  835.9 15.5 %collective-permute-start.3 = (bf16[1,16,16,512]{3,2,1,0:T(8,128)(2,1)S(1)}, bf16[1,16,16,512]{3,2,1,0:T(8,128)(2,1)S(1)}, u32[]{:S(2)}, u32[]{:S(2)}) collective-permute-start(bf16[1,16,16,512]{3,2,1,0:T(8,128)(2,1)S(1)} %collective-permute-done.2), channel_id=1, source_target_pairs={{0,128},{32,160},{64,192},{96,224},{128,0},{160,32},{192,64},{224,... | collective-permute-start | bytes 786440 | tf_op jit(solution)/shard_map/while/body/eval_jaxpr/ppermute | solution.py:16
  875.7 92.0 %all-reduce.4.cloned.1.call-done = bf16[4,1,16,16,512]{4,3,2,1,0:T(8,128)(2,1)} async-done(((bf16[4,1,16,16,512]{4,3,2,1,0:T(8,128)(2,1)}), bf16[4,1,16,16,512]{4,3,2,1,0:T(8,128)(2,1)}) %all-reduce.4.cloned.1.call-update) | async-done | bytes 1048592 | tf_op jit(solution)/shard_map/psum | solution.py:38
  (352 shorter events, 490.3 us)
Async XLA Ops:
  6.5 58.5 %all-gather.8.cloned.1.call-start = ((), (), s32[]{:S(2)}) async-start(), calls=%async_computation.2 | async-start | bytes 1622016 | tf_op jit(solution)/shard_map/all_gather | solution.py:75
  7.3 121.2 %all-gather.4.cloned.1.call-start = ((), (), s32[]{:S(2)}) async-start(), calls=%async_computation | async-start | bytes 4866048 | tf_op jit(solution)/shard_map/all_gather | solution.py:73
  8.0 183.6 %all-gather.6.cloned.1.call-start = ((), (), s32[]{:S(2)}) async-start(), calls=%async_computation.1 | async-start | bytes 4866048 | tf_op jit(solution)/shard_map/all_gather | solution.py:74
  8.7 959.0 %all-reduce.4.cloned.1.call-start = ((), (), s32[]{:S(2)}) async-start(), calls=%async_computation.3 | async-start | bytes 2097152 | tf_op jit(solution)/shard_map/psum | solution.py:38
  233.0 10.7 %collective-permute-start.4 = (bf16[1,16,16,512]{3,2,1,0:T(8,128)(2,1)S(1)}, bf16[1,16,16,512]{3,2,1,0:T(8,128)(2,1)S(1)}, u32[]{:S(2)}, u32[]{:S(2)}) collective-permute-start(bf16[1,16,16,512]{3,2,1,0:T(8,128)(2,1)S(1)} %get-tuple-element.378), channel_id=1, source_target_pairs={{0,1},{1,2},{2,3},{3,4},{4,5},{5,6},{6,7},{7,8},{8,9},{9,10},{10,1... | collective-permute-start | bytes 786440 | tf_op jit(solution)/shard_map/while/body/eval_jaxpr/ppermute | solution.py:27
  292.0 10.9 %collective-permute-start.4 = (bf16[1,16,16,512]{3,2,1,0:T(8,128)(2,1)S(1)}, bf16[1,16,16,512]{3,2,1,0:T(8,128)(2,1)S(1)}, u32[]{:S(2)}, u32[]{:S(2)}) collective-permute-start(bf16[1,16,16,512]{3,2,1,0:T(8,128)(2,1)S(1)} %get-tuple-element.378), channel_id=1, source_target_pairs={{0,1},{1,2},{2,3},{3,4},{4,5},{5,6},{6,7},{7,8},{8,9},{9,10},{10,1... | collective-permute-start | bytes 786440 | tf_op jit(solution)/shard_map/while/body/eval_jaxpr/ppermute | solution.py:27
  293.9 13.4 %collective-permute-start.5 = (bf16[1,16,16,512]{3,2,1,0:T(8,128)(2,1)S(1)}, bf16[1,16,16,512]{3,2,1,0:T(8,128)(2,1)S(1)}, u32[]{:S(2)}, u32[]{:S(2)}) collective-permute-start(bf16[1,16,16,512]{3,2,1,0:T(8,128)(2,1)S(1)} %get-tuple-element.378), channel_id=1, source_target_pairs={{1,0},{2,1},{3,2},{4,3},{5,4},{6,5},{7,6},{8,7},{9,8},{10,9},{11,1... | collective-permute-start | bytes 786440 | tf_op jit(solution)/shard_map/while/body/eval_jaxpr/ppermute | solution.py:29
  355.3 10.8 %collective-permute-start.4 = (bf16[1,16,16,512]{3,2,1,0:T(8,128)(2,1)S(1)}, bf16[1,16,16,512]{3,2,1,0:T(8,128)(2,1)S(1)}, u32[]{:S(2)}, u32[]{:S(2)}) collective-permute-start(bf16[1,16,16,512]{3,2,1,0:T(8,128)(2,1)S(1)} %get-tuple-element.378), channel_id=1, source_target_pairs={{0,1},{1,2},{2,3},{3,4},{4,5},{5,6},{6,7},{7,8},{8,9},{9,10},{10,1... | collective-permute-start | bytes 786440 | tf_op jit(solution)/shard_map/while/body/eval_jaxpr/ppermute | solution.py:27
  357.3 13.4 %collective-permute-start.5 = (bf16[1,16,16,512]{3,2,1,0:T(8,128)(2,1)S(1)}, bf16[1,16,16,512]{3,2,1,0:T(8,128)(2,1)S(1)}, u32[]{:S(2)}, u32[]{:S(2)}) collective-permute-start(bf16[1,16,16,512]{3,2,1,0:T(8,128)(2,1)S(1)} %get-tuple-element.378), channel_id=1, source_target_pairs={{1,0},{2,1},{3,2},{4,3},{5,4},{6,5},{7,6},{8,7},{9,8},{10,9},{11,1... | collective-permute-start | bytes 786440 | tf_op jit(solution)/shard_map/while/body/eval_jaxpr/ppermute | solution.py:29
  419.2 10.8 %collective-permute-start.4 = (bf16[1,16,16,512]{3,2,1,0:T(8,128)(2,1)S(1)}, bf16[1,16,16,512]{3,2,1,0:T(8,128)(2,1)S(1)}, u32[]{:S(2)}, u32[]{:S(2)}) collective-permute-start(bf16[1,16,16,512]{3,2,1,0:T(8,128)(2,1)S(1)} %get-tuple-element.378), channel_id=1, source_target_pairs={{0,1},{1,2},{2,3},{3,4},{4,5},{5,6},{6,7},{7,8},{8,9},{9,10},{10,1... | collective-permute-start | bytes 786440 | tf_op jit(solution)/shard_map/while/body/eval_jaxpr/ppermute | solution.py:27
  421.2 13.3 %collective-permute-start.5 = (bf16[1,16,16,512]{3,2,1,0:T(8,128)(2,1)S(1)}, bf16[1,16,16,512]{3,2,1,0:T(8,128)(2,1)S(1)}, u32[]{:S(2)}, u32[]{:S(2)}) collective-permute-start(bf16[1,16,16,512]{3,2,1,0:T(8,128)(2,1)S(1)} %get-tuple-element.378), channel_id=1, source_target_pairs={{1,0},{2,1},{3,2},{4,3},{5,4},{6,5},{7,6},{8,7},{9,8},{10,9},{11,1... | collective-permute-start | bytes 786440 | tf_op jit(solution)/shard_map/while/body/eval_jaxpr/ppermute | solution.py:29
  476.5 10.7 %collective-permute-start.4 = (bf16[1,16,16,512]{3,2,1,0:T(8,128)(2,1)S(1)}, bf16[1,16,16,512]{3,2,1,0:T(8,128)(2,1)S(1)}, u32[]{:S(2)}, u32[]{:S(2)}) collective-permute-start(bf16[1,16,16,512]{3,2,1,0:T(8,128)(2,1)S(1)} %get-tuple-element.378), channel_id=1, source_target_pairs={{0,1},{1,2},{2,3},{3,4},{4,5},{5,6},{6,7},{7,8},{8,9},{9,10},{10,1... | collective-permute-start | bytes 786440 | tf_op jit(solution)/shard_map/while/body/eval_jaxpr/ppermute | solution.py:27
  491.1 18.7 %collective-permute-start = (bf16[1,16,16,512]{3,2,1,0:T(8,128)(2,1)}, bf16[1,16,16,512]{3,2,1,0:T(8,128)(2,1)S(1)}, u32[]{:S(2)}, u32[]{:S(2)}) collective-permute-start(bf16[1,16,16,512]{3,2,1,0:T(8,128)(2,1)} %get-tuple-element.343), channel_id=1, source_target_pairs={{0,32},{32,64},{64,96},{96,128},{128,160},{160,192},{192,224},{1,3... | collective-permute-start | bytes 786440 | tf_op jit(solution)/shard_map/while/body/eval_jaxpr/ppermute | solution.py:12
  510.8 11.3 %collective-permute-start.1 = (bf16[1,16,16,512]{3,2,1,0:T(8,128)(2,1)S(1)}, bf16[1,16,16,512]{3,2,1,0:T(8,128)(2,1)S(1)}, u32[]{:S(2)}, u32[]{:S(2)}) collective-permute-start(bf16[1,16,16,512]{3,2,1,0:T(8,128)(2,1)S(1)} %bitcast_select_fusion.2), channel_id=1, source_target_pairs={{0,32},{32,0},{64,96},{96,64},{128,160},{160,128},{192,224},{224,1... | collective-permute-start | bytes 786440 | tf_op jit(solution)/shard_map/while/body/eval_jaxpr/ppermute | solution.py:16
  538.7 10.8 %collective-permute-start.4 = (bf16[1,16,16,512]{3,2,1,0:T(8,128)(2,1)S(1)}, bf16[1,16,16,512]{3,2,1,0:T(8,128)(2,1)S(1)}, u32[]{:S(2)}, u32[]{:S(2)}) collective-permute-start(bf16[1,16,16,512]{3,2,1,0:T(8,128)(2,1)S(1)} %get-tuple-element.378), channel_id=1, source_target_pairs={{0,1},{1,2},{2,3},{3,4},{4,5},{5,6},{6,7},{7,8},{8,9},{9,10},{10,1... | collective-permute-start | bytes 786440 | tf_op jit(solution)/shard_map/while/body/eval_jaxpr/ppermute | solution.py:27
  540.6 13.0 %collective-permute-start.5 = (bf16[1,16,16,512]{3,2,1,0:T(8,128)(2,1)S(1)}, bf16[1,16,16,512]{3,2,1,0:T(8,128)(2,1)S(1)}, u32[]{:S(2)}, u32[]{:S(2)}) collective-permute-start(bf16[1,16,16,512]{3,2,1,0:T(8,128)(2,1)S(1)} %get-tuple-element.378), channel_id=1, source_target_pairs={{1,0},{2,1},{3,2},{4,3},{5,4},{6,5},{7,6},{8,7},{9,8},{10,9},{11,1... | collective-permute-start | bytes 786440 | tf_op jit(solution)/shard_map/while/body/eval_jaxpr/ppermute | solution.py:29
  562.9 21.5 %collective-permute-start.1 = (bf16[1,16,16,512]{3,2,1,0:T(8,128)(2,1)S(1)}, bf16[1,16,16,512]{3,2,1,0:T(8,128)(2,1)S(1)}, u32[]{:S(2)}, u32[]{:S(2)}) collective-permute-start(bf16[1,16,16,512]{3,2,1,0:T(8,128)(2,1)S(1)} %bitcast_select_fusion.2), channel_id=1, source_target_pairs={{0,32},{32,0},{64,96},{96,64},{128,160},{160,128},{192,224},{224,1... | collective-permute-start | bytes 786440 | tf_op jit(solution)/shard_map/while/body/eval_jaxpr/ppermute | solution.py:16
  601.8 10.8 %collective-permute-start.4 = (bf16[1,16,16,512]{3,2,1,0:T(8,128)(2,1)S(1)}, bf16[1,16,16,512]{3,2,1,0:T(8,128)(2,1)S(1)}, u32[]{:S(2)}, u32[]{:S(2)}) collective-permute-start(bf16[1,16,16,512]{3,2,1,0:T(8,128)(2,1)S(1)} %get-tuple-element.378), channel_id=1, source_target_pairs={{0,1},{1,2},{2,3},{3,4},{4,5},{5,6},{6,7},{7,8},{8,9},{9,10},{10,1... | collective-permute-start | bytes 786440 | tf_op jit(solution)/shard_map/while/body/eval_jaxpr/ppermute | solution.py:27
  603.8 12.2 %collective-permute-start.5 = (bf16[1,16,16,512]{3,2,1,0:T(8,128)(2,1)S(1)}, bf16[1,16,16,512]{3,2,1,0:T(8,128)(2,1)S(1)}, u32[]{:S(2)}, u32[]{:S(2)}) collective-permute-start(bf16[1,16,16,512]{3,2,1,0:T(8,128)(2,1)S(1)} %get-tuple-element.378), channel_id=1, source_target_pairs={{1,0},{2,1},{3,2},{4,3},{5,4},{6,5},{7,6},{8,7},{9,8},{10,9},{11,1... | collective-permute-start | bytes 786440 | tf_op jit(solution)/shard_map/while/body/eval_jaxpr/ppermute | solution.py:29
  637.9 16.8 %collective-permute-start.2 = (bf16[1,16,16,512]{3,2,1,0:T(8,128)(2,1)S(1)}, bf16[1,16,16,512]{3,2,1,0:T(8,128)(2,1)S(1)}, u32[]{:S(2)}, u32[]{:S(2)}) collective-permute-start(bf16[1,16,16,512]{3,2,1,0:T(8,128)(2,1)S(1)} %collective-permute-done.1), channel_id=1, source_target_pairs={{0,64},{32,96},{64,0},{96,32},{128,192},{160,224},{192,128},{224,1... | collective-permute-start | bytes 786440 | tf_op jit(solution)/shard_map/while/body/eval_jaxpr/ppermute | solution.py:16
  664.9 10.8 %collective-permute-start.4 = (bf16[1,16,16,512]{3,2,1,0:T(8,128)(2,1)S(1)}, bf16[1,16,16,512]{3,2,1,0:T(8,128)(2,1)S(1)}, u32[]{:S(2)}, u32[]{:S(2)}) collective-permute-start(bf16[1,16,16,512]{3,2,1,0:T(8,128)(2,1)S(1)} %get-tuple-element.378), channel_id=1, source_target_pairs={{0,1},{1,2},{2,3},{3,4},{4,5},{5,6},{6,7},{7,8},{8,9},{9,10},{10,1... | collective-permute-start | bytes 786440 | tf_op jit(solution)/shard_map/while/body/eval_jaxpr/ppermute | solution.py:27
  666.8 10.7 %collective-permute-start.5 = (bf16[1,16,16,512]{3,2,1,0:T(8,128)(2,1)S(1)}, bf16[1,16,16,512]{3,2,1,0:T(8,128)(2,1)S(1)}, u32[]{:S(2)}, u32[]{:S(2)}) collective-permute-start(bf16[1,16,16,512]{3,2,1,0:T(8,128)(2,1)S(1)} %get-tuple-element.378), channel_id=1, source_target_pairs={{1,0},{2,1},{3,2},{4,3},{5,4},{6,5},{7,6},{8,7},{9,8},{10,9},{11,1... | collective-permute-start | bytes 786440 | tf_op jit(solution)/shard_map/while/body/eval_jaxpr/ppermute | solution.py:29
  679.6 10.7 %collective-permute-start = (bf16[1,16,16,512]{3,2,1,0:T(8,128)(2,1)}, bf16[1,16,16,512]{3,2,1,0:T(8,128)(2,1)S(1)}, u32[]{:S(2)}, u32[]{:S(2)}) collective-permute-start(bf16[1,16,16,512]{3,2,1,0:T(8,128)(2,1)} %get-tuple-element.343), channel_id=1, source_target_pairs={{0,32},{32,64},{64,96},{96,128},{128,160},{160,192},{192,224},{1,3... | collective-permute-start | bytes 786440 | tf_op jit(solution)/shard_map/while/body/eval_jaxpr/ppermute | solution.py:12
  699.2 17.3 %collective-permute-start.2 = (bf16[1,16,16,512]{3,2,1,0:T(8,128)(2,1)S(1)}, bf16[1,16,16,512]{3,2,1,0:T(8,128)(2,1)S(1)}, u32[]{:S(2)}, u32[]{:S(2)}) collective-permute-start(bf16[1,16,16,512]{3,2,1,0:T(8,128)(2,1)S(1)} %collective-permute-done.1), channel_id=1, source_target_pairs={{0,64},{32,96},{64,0},{96,32},{128,192},{160,224},{192,128},{224,1... | collective-permute-start | bytes 786440 | tf_op jit(solution)/shard_map/while/body/eval_jaxpr/ppermute | solution.py:16
  727.6 10.8 %collective-permute-start.4 = (bf16[1,16,16,512]{3,2,1,0:T(8,128)(2,1)S(1)}, bf16[1,16,16,512]{3,2,1,0:T(8,128)(2,1)S(1)}, u32[]{:S(2)}, u32[]{:S(2)}) collective-permute-start(bf16[1,16,16,512]{3,2,1,0:T(8,128)(2,1)S(1)} %get-tuple-element.378), channel_id=1, source_target_pairs={{0,1},{1,2},{2,3},{3,4},{4,5},{5,6},{6,7},{7,8},{8,9},{9,10},{10,1... | collective-permute-start | bytes 786440 | tf_op jit(solution)/shard_map/while/body/eval_jaxpr/ppermute | solution.py:27
  729.6 13.1 %collective-permute-start.5 = (bf16[1,16,16,512]{3,2,1,0:T(8,128)(2,1)S(1)}, bf16[1,16,16,512]{3,2,1,0:T(8,128)(2,1)S(1)}, u32[]{:S(2)}, u32[]{:S(2)}) collective-permute-start(bf16[1,16,16,512]{3,2,1,0:T(8,128)(2,1)S(1)} %get-tuple-element.378), channel_id=1, source_target_pairs={{1,0},{2,1},{3,2},{4,3},{5,4},{6,5},{7,6},{8,7},{9,8},{10,9},{11,1... | collective-permute-start | bytes 786440 | tf_op jit(solution)/shard_map/while/body/eval_jaxpr/ppermute | solution.py:29
  767.6 23.5 %collective-permute-start.3 = (bf16[1,16,16,512]{3,2,1,0:T(8,128)(2,1)S(1)}, bf16[1,16,16,512]{3,2,1,0:T(8,128)(2,1)S(1)}, u32[]{:S(2)}, u32[]{:S(2)}) collective-permute-start(bf16[1,16,16,512]{3,2,1,0:T(8,128)(2,1)S(1)} %collective-permute-done.2), channel_id=1, source_target_pairs={{0,128},{32,160},{64,192},{96,224},{128,0},{160,32},{192,64},{224,... | collective-permute-start | bytes 786440 | tf_op jit(solution)/shard_map/while/body/eval_jaxpr/ppermute | solution.py:16
  791.7 10.8 %collective-permute-start.4 = (bf16[1,16,16,512]{3,2,1,0:T(8,128)(2,1)S(1)}, bf16[1,16,16,512]{3,2,1,0:T(8,128)(2,1)S(1)}, u32[]{:S(2)}, u32[]{:S(2)}) collective-permute-start(bf16[1,16,16,512]{3,2,1,0:T(8,128)(2,1)S(1)} %get-tuple-element.378), channel_id=1, source_target_pairs={{0,1},{1,2},{2,3},{3,4},{4,5},{5,6},{6,7},{7,8},{8,9},{9,10},{10,1... | collective-permute-start | bytes 786440 | tf_op jit(solution)/shard_map/while/body/eval_jaxpr/ppermute | solution.py:27
  793.6 13.3 %collective-permute-start.5 = (bf16[1,16,16,512]{3,2,1,0:T(8,128)(2,1)S(1)}, bf16[1,16,16,512]{3,2,1,0:T(8,128)(2,1)S(1)}, u32[]{:S(2)}, u32[]{:S(2)}) collective-permute-start(bf16[1,16,16,512]{3,2,1,0:T(8,128)(2,1)S(1)} %get-tuple-element.378), channel_id=1, source_target_pairs={{1,0},{2,1},{3,2},{4,3},{5,4},{6,5},{7,6},{8,7},{9,8},{10,9},{11,1... | collective-permute-start | bytes 786440 | tf_op jit(solution)/shard_map/while/body/eval_jaxpr/ppermute | solution.py:29
  835.9 20.8 %collective-permute-start.3 = (bf16[1,16,16,512]{3,2,1,0:T(8,128)(2,1)S(1)}, bf16[1,16,16,512]{3,2,1,0:T(8,128)(2,1)S(1)}, u32[]{:S(2)}, u32[]{:S(2)}) collective-permute-start(bf16[1,16,16,512]{3,2,1,0:T(8,128)(2,1)S(1)} %collective-permute-done.2), channel_id=1, source_target_pairs={{0,128},{32,160},{64,192},{96,224},{128,0},{160,32},{192,64},{224,... | collective-permute-start | bytes 786440 | tf_op jit(solution)/shard_map/while/body/eval_jaxpr/ppermute | solution.py:16
  857.3 10.8 %collective-permute-start.4 = (bf16[1,16,16,512]{3,2,1,0:T(8,128)(2,1)S(1)}, bf16[1,16,16,512]{3,2,1,0:T(8,128)(2,1)S(1)}, u32[]{:S(2)}, u32[]{:S(2)}) collective-permute-start(bf16[1,16,16,512]{3,2,1,0:T(8,128)(2,1)S(1)} %get-tuple-element.378), channel_id=1, source_target_pairs={{0,1},{1,2},{2,3},{3,4},{4,5},{5,6},{6,7},{7,8},{8,9},{9,10},{10,1... | collective-permute-start | bytes 786440 | tf_op jit(solution)/shard_map/while/body/eval_jaxpr/ppermute | solution.py:27
  859.2 13.3 %collective-permute-start.5 = (bf16[1,16,16,512]{3,2,1,0:T(8,128)(2,1)S(1)}, bf16[1,16,16,512]{3,2,1,0:T(8,128)(2,1)S(1)}, u32[]{:S(2)}, u32[]{:S(2)}) collective-permute-start(bf16[1,16,16,512]{3,2,1,0:T(8,128)(2,1)S(1)} %get-tuple-element.378), channel_id=1, source_target_pairs={{1,0},{2,1},{3,2},{4,3},{5,4},{6,5},{7,6},{8,7},{9,8},{10,9},{11,1... | collective-permute-start | bytes 786440 | tf_op jit(solution)/shard_map/while/body/eval_jaxpr/ppermute | solution.py:29
  (50 other events, 349.6 us)
Sparse Core Ops, SparseCore 0:
  10.0 55.0 all-gather.7
  67.7 60.6 all-gather.3
  131.1 60.4 all-gather.5
  875.8 91.8 all-reduce.3
where the time goes:
time: 978 us; the launch traced here: 976 us
  waiting for transfers between devices  577 us (59%)
  starting transfers between devices  273 us (28%)
  matrix products  46.2 us (5%)
  other arithmetic  32.5 us (3%)
  loops' own time  17.3 us (2%)
  local copies, waits for them, and re-layouts  17 us (2%)
  between operations  13.2 us (1%)
    ppermute x33, waiting for transfers between devices, partner(): lax.ppermute(shard, axis, [(i, i ^ 1 << bit) for i in range(lax.axis_size...  190 us
    ppermute x33, starting transfers between devices, partner(): lax.ppermute(shard, axis, [(i, i ^ 1 << bit) for i in range(lax.axis_size...  141 us
    psum x1, waiting for transfers between devices, broadcast(): return lax.psum(jnp.where(mine, shard, jnp.zeros_like(shard)), axis)  92 us
    ppermute x11, starting transfers between devices, extended_2(): lax.ppermute(head, axis, [((i + 1) % count, i) for i in range(ends)])  73.2 us
    all_gather x1, waiting for transfers between devices, on_device(): lax.all_gather(conv_first, 'frame', axis=2, tiled=True)  63.4 us
    all_gather x1, waiting for transfers between devices, on_device(): lax.all_gather(conv_second, 'frame', axis=2, tiled=True)  63.1 us
    all_gather x1, waiting for transfers between devices, on_device(): lax.all_gather(temporal, 'frame', axis=2, tiled=True)  56.3 us
    ppermute x11, waiting for transfers between devices, passed_along(): return lax.ppermute(shard, axis, pairs)  47.2 us
  transfers between devices with their start and end apart: 70, of which 70 were waited for; matrix products, arithmetic and copies ran while one was open for 1% of the time, Pallas kernels for 0%

commit v1 on v0

--- a/solution.py
+++ b/solution.py
@@ -35,7 +35,7 @@
 
 def broadcast(shard, axis, root):
     mine = lax.axis_index(axis) == root
-    return lax.psum(jnp.where(mine, shard, jnp.zeros_like(shard)), axis)
+    return jnp.sum(lax.all_gather(jnp.where(mine, shard, jnp.zeros_like(shard)), axis), axis=0)
 
 
 def spatial(field_in, kernel):

time: 978 us -> 1070 us (1.094)
  waiting for transfers between devices: 577 us -> 663 us
    all_gather x0 -> x1, waiting for transfers between devices: none -> 178 us  [broadcast(): lax.all_gather(jnp.where(mine, shard, jnp.zeros_like(shard)), axis)]
    psum x1 -> x0, waiting for transfers between devices: 92 us -> none  [broadcast(): return lax.psum(jnp.where(mine, shard, jnp.zeros_like(shard)), axis)]
where the time goes in v1:
time: 1070 us
  waiting for transfers between devices  663 us (62%)
  starting transfers between devices  273 us (26%)
  matrix products  46.2 us (4%)
  other arithmetic  38.1 us (4%)
  loops' own time  17.3 us (2%)
  local copies, waits for them, and re-layouts  16.1 us (2%)
  between operations  13.2 us (1%)
    ppermute x33, waiting for transfers between devices, partner(): lax.ppermute(shard, axis, [(i, i ^ 1 << bit) for i in range(lax.axis_size...  190 us
    all_gather x1, waiting for transfers between devices, broadcast(): lax.all_gather(jnp.where(mine, shard, jnp.zeros_like(shard)), axis)  178 us
    ppermute x33, starting transfers between devices, partner(): lax.ppermute(shard, axis, [(i, i ^ 1 << bit) for i in range(lax.axis_size...  141 us
    ppermute x11, starting transfers between devices, extended_2(): lax.ppermute(head, axis, [((i + 1) % count, i) for i in range(ends)])  73.2 us
    all_gather x1, waiting for transfers between devices, on_device(): lax.all_gather(conv_first, 'frame', axis=2, tiled=True)  63.4 us
    all_gather x1, waiting for transfers between devices, on_device(): lax.all_gather(conv_second, 'frame', axis=2, tiled=True)  63.1 us
    all_gather x1, waiting for transfers between devices, on_device(): lax.all_gather(temporal, 'frame', axis=2, tiled=True)  56.3 us
    ppermute x11, waiting for transfers between devices, passed_along(): return lax.ppermute(shard, axis, pairs)  47.2 us
  transfers between devices with their start and end apart: 70, of which 70 were waited for; matrix products, arithmetic and copies ran while one was open for 1% of the time, Pallas kernels for 0%

profile of v1, /device:TPU:2, one launch (start us, length us, event | category | flops | bytes accessed | tf_op | source)
XLA Modules:
  0.0 1066.2 jit_solution(9618768710059821589)
XLA Ops:
  8.8 56.3 %all-gather.10.cloned.1.call-done = bf16[1,3,512,512]{3,2,1,0:T(8,128)(2,1)} async-done(((bf16[1,3,16,512]{3,2,1,0:T(8,128)(2,1)}), bf16[1,3,512,512]{3,2,1,0:T(8,128)(2,1)}) %all-gather.10.cloned.1.call-update) | async-done | bytes 1572880 | tf_op jit(solution)/shard_map/all_gather | solution.py:75
  65.1 63.4 %all-gather.6.cloned.1.call-done = bf16[1,9,512,512]{3,2,1,0:T(8,128)(2,1)} async-done(((bf16[1,9,16,512]{3,2,1,0:T(8,128)(2,1)}), bf16[1,9,512,512]{3,2,1,0:T(8,128)(2,1)}) %all-gather.6.cloned.1.call-update) | async-done | bytes 4718608 | tf_op jit(solution)/shard_map/all_gather | solution.py:73
  128.4 63.1 %all-gather.8.cloned.1.call-done = bf16[1,9,512,512]{3,2,1,0:T(8,128)(2,1)} async-done(((bf16[1,9,16,512]{3,2,1,0:T(8,128)(2,1)}), bf16[1,9,512,512]{3,2,1,0:T(8,128)(2,1)}) %all-gather.8.cloned.1.call-update) | async-done | bytes 4718608 | tf_op jit(solution)/shard_map/all_gather | solution.py:74
  192.3 682.3 %while.16 = (s32[]{:T(128)}, bf16[1,16,16,512]{3,2,1,0:T(8,128)(2,1)}, bf16[4,1,16,16,512]{4,3,2,1,0:T(8,128)(2,1)S(1)}, bf16[4,1,16,16,512]{4,3,2,1,0:T(8,128)(...) while((s32[]{:T(128)}, ...), condition=%wide.region_5.6_spmd.clone, body=%wide.region_0.5_spmd.clone.sunk | while | flops 2825650176 | bytes 99615424 | solution.py:128
  234.9 6.7 collective-permute-start.5
  245.5 7.0 conditional.7
  270.5 7.6 collective-permute-done.2
  278.8 7.2 collective-permute-done.3
  293.9 6.7 collective-permute-start.5
  307.3 7.0 conditional.7
  342.1 7.3 collective-permute-done.3
  357.3 6.7 collective-permute-start.5
  370.6 7.0 conditional.7
  397.8 7.7 collective-permute-done.2
  406.1 7.2 collective-permute-done.3
  421.2 6.7 collective-permute-start.5
  434.5 7.0 conditional.7
  468.4 7.5 collective-permute-done.3
  478.5 6.7 collective-permute-start.5
  491.1 14.6 %collective-permute-start = (bf16[1,16,16,512]{3,2,1,0:T(8,128)(2,1)}, bf16[1,16,16,512]{3,2,1,0:T(8,128)(2,1)S(1)}, u32[]{:S(2)}, u32[]{:S(2)}) collective-permute-start(bf16[1,16,16,512]{3,2,1,0:T(8,128)(2,1)} %get-tuple-element.343), channel_id=1, source_target_pairs={{0,32},{32,64},{64,96},{96,128},{128,160},{160,192},{192,224},{1,3... | collective-permute-start | bytes 786440 | tf_op jit(solution)/shard_map/while/body/eval_jaxpr/ppermute | solution.py:12
  510.8 6.9 collective-permute-start.1
  531.0 7.2 collective-permute-done.3
  562.9 15.2 %collective-permute-start.1 = (bf16[1,16,16,512]{3,2,1,0:T(8,128)(2,1)S(1)}, bf16[1,16,16,512]{3,2,1,0:T(8,128)(2,1)S(1)}, u32[]{:S(2)}, u32[]{:S(2)}) collective-permute-start(bf16[1,16,16,512]{3,2,1,0:T(8,128)(2,1)S(1)} %bitcast_select_fusion.2), channel_id=1, source_target_pairs={{0,32},{32,0},{64,96},{96,64},{128,160},{160,128},{192,224},{224,1... | collective-permute-start | bytes 786440 | tf_op jit(solution)/shard_map/while/body/eval_jaxpr/ppermute | solution.py:16
  594.0 7.3 collective-permute-done.3
  603.8 6.7 collective-permute-start.5
  637.9 11.0 %collective-permute-start.2 = (bf16[1,16,16,512]{3,2,1,0:T(8,128)(2,1)S(1)}, bf16[1,16,16,512]{3,2,1,0:T(8,128)(2,1)S(1)}, u32[]{:S(2)}, u32[]{:S(2)}) collective-permute-start(bf16[1,16,16,512]{3,2,1,0:T(8,128)(2,1)S(1)} %collective-permute-done.1), channel_id=1, source_target_pairs={{0,64},{32,96},{64,0},{96,32},{128,192},{160,224},{192,128},{224,1... | collective-permute-start | bytes 786440 | tf_op jit(solution)/shard_map/while/body/eval_jaxpr/ppermute | solution.py:16
  666.8 6.7 collective-permute-start.5
  699.2 13.0 %collective-permute-start.2 = (bf16[1,16,16,512]{3,2,1,0:T(8,128)(2,1)S(1)}, bf16[1,16,16,512]{3,2,1,0:T(8,128)(2,1)S(1)}, u32[]{:S(2)}, u32[]{:S(2)}) collective-permute-start(bf16[1,16,16,512]{3,2,1,0:T(8,128)(2,1)S(1)} %collective-permute-done.1), channel_id=1, source_target_pairs={{0,64},{32,96},{64,0},{96,32},{128,192},{160,224},{192,128},{224,1... | collective-permute-start | bytes 786440 | tf_op jit(solution)/shard_map/while/body/eval_jaxpr/ppermute | solution.py:16
  767.6 19.2 %collective-permute-start.3 = (bf16[1,16,16,512]{3,2,1,0:T(8,128)(2,1)S(1)}, bf16[1,16,16,512]{3,2,1,0:T(8,128)(2,1)S(1)}, u32[]{:S(2)}, u32[]{:S(2)}) collective-permute-start(bf16[1,16,16,512]{3,2,1,0:T(8,128)(2,1)S(1)} %collective-permute-done.2), channel_id=1, source_target_pairs={{0,128},{32,160},{64,192},{96,224},{128,0},{160,32},{192,64},{224,... | collective-permute-start | bytes 786440 | tf_op jit(solution)/shard_map/while/body/eval_jaxpr/ppermute | solution.py:16
  793.6 6.7 collective-permute-start.5
  835.9 15.5 %collective-permute-start.3 = (bf16[1,16,16,512]{3,2,1,0:T(8,128)(2,1)S(1)}, bf16[1,16,16,512]{3,2,1,0:T(8,128)(2,1)S(1)}, u32[]{:S(2)}, u32[]{:S(2)}) collective-permute-start(bf16[1,16,16,512]{3,2,1,0:T(8,128)(2,1)S(1)} %collective-permute-done.2), channel_id=1, source_target_pairs={{0,128},{32,160},{64,192},{96,224},{128,0},{160,32},{192,64},{224,... | collective-permute-start | bytes 786440 | tf_op jit(solution)/shard_map/while/body/eval_jaxpr/ppermute | solution.py:16
  875.8 177.7 %all-gather.12.cloned.1.call-done = bf16[32,1,16,16,512]{4,3,2,1,0:T(8,128)(2,1)} async-done(((bf16[4,1,16,16,512]{4,3,2,1,0:T(8,128)(2,1)}), bf16[32,1,16,16,512]{4,3,2,1,0:T(8,128)(2,1)}) %all-gather.12.cloned.1.call-update) | async-done | bytes 8388624 | tf_op jit(solution)/shard_map/all_gather | solution.py:38
  (353 shorter events, 494.9 us)
Async XLA Ops:
  6.5 58.5 %all-gather.10.cloned.1.call-start = ((), (), s32[]{:S(2)}) async-start(), calls=%async_computation.2 | async-start | bytes 1622016 | tf_op jit(solution)/shard_map/all_gather | solution.py:75
  7.3 121.2 %all-gather.6.cloned.1.call-start = ((), (), s32[]{:S(2)}) async-start(), calls=%async_computation | async-start | bytes 4866048 | tf_op jit(solution)/shard_map/all_gather | solution.py:73
  8.0 183.6 %all-gather.8.cloned.1.call-start = ((), (), s32[]{:S(2)}) async-start(), calls=%async_computation.1 | async-start | bytes 4866048 | tf_op jit(solution)/shard_map/all_gather | solution.py:74
  8.7 1044.8 %all-gather.12.cloned.1.call-start = ((), (), s32[]{:S(2)}) async-start(), calls=%async_computation.3 | async-start | bytes 9437184 | tf_op jit(solution)/shard_map/all_gather | solution.py:38
  233.0 10.7 %collective-permute-start.4 = (bf16[1,16,16,512]{3,2,1,0:T(8,128)(2,1)S(1)}, bf16[1,16,16,512]{3,2,1,0:T(8,128)(2,1)S(1)}, u32[]{:S(2)}, u32[]{:S(2)}) collective-permute-start(bf16[1,16,16,512]{3,2,1,0:T(8,128)(2,1)S(1)} %get-tuple-element.378), channel_id=1, source_target_pairs={{0,1},{1,2},{2,3},{3,4},{4,5},{5,6},{6,7},{7,8},{8,9},{9,10},{10,1... | collective-permute-start | bytes 786440 | tf_op jit(solution)/shard_map/while/body/eval_jaxpr/ppermute | solution.py:27
  292.0 10.9 %collective-permute-start.4 = (bf16[1,16,16,512]{3,2,1,0:T(8,128)(2,1)S(1)}, bf16[1,16,16,512]{3,2,1,0:T(8,128)(2,1)S(1)}, u32[]{:S(2)}, u32[]{:S(2)}) collective-permute-start(bf16[1,16,16,512]{3,2,1,0:T(8,128)(2,1)S(1)} %get-tuple-element.378), channel_id=1, source_target_pairs={{0,1},{1,2},{2,3},{3,4},{4,5},{5,6},{6,7},{7,8},{8,9},{9,10},{10,1... | collective-permute-start | bytes 786440 | tf_op jit(solution)/shard_map/while/body/eval_jaxpr/ppermute | solution.py:27
  293.9 13.4 %collective-permute-start.5 = (bf16[1,16,16,512]{3,2,1,0:T(8,128)(2,1)S(1)}, bf16[1,16,16,512]{3,2,1,0:T(8,128)(2,1)S(1)}, u32[]{:S(2)}, u32[]{:S(2)}) collective-permute-start(bf16[1,16,16,512]{3,2,1,0:T(8,128)(2,1)S(1)} %get-tuple-element.378), channel_id=1, source_target_pairs={{1,0},{2,1},{3,2},{4,3},{5,4},{6,5},{7,6},{8,7},{9,8},{10,9},{11,1... | collective-permute-start | bytes 786440 | tf_op jit(solution)/shard_map/while/body/eval_jaxpr/ppermute | solution.py:29
  355.3 10.8 %collective-permute-start.4 = (bf16[1,16,16,512]{3,2,1,0:T(8,128)(2,1)S(1)}, bf16[1,16,16,512]{3,2,1,0:T(8,128)(2,1)S(1)}, u32[]{:S(2)}, u32[]{:S(2)}) collective-permute-start(bf16[1,16,16,512]{3,2,1,0:T(8,128)(2,1)S(1)} %get-tuple-element.378), channel_id=1, source_target_pairs={{0,1},{1,2},{2,3},{3,4},{4,5},{5,6},{6,7},{7,8},{8,9},{9,10},{10,1... | collective-permute-start | bytes 786440 | tf_op jit(solution)/shard_map/while/body/eval_jaxpr/ppermute | solution.py:27
  357.3 13.4 %collective-permute-start.5 = (bf16[1,16,16,512]{3,2,1,0:T(8,128)(2,1)S(1)}, bf16[1,16,16,512]{3,2,1,0:T(8,128)(2,1)S(1)}, u32[]{:S(2)}, u32[]{:S(2)}) collective-permute-start(bf16[1,16,16,512]{3,2,1,0:T(8,128)(2,1)S(1)} %get-tuple-element.378), channel_id=1, source_target_pairs={{1,0},{2,1},{3,2},{4,3},{5,4},{6,5},{7,6},{8,7},{9,8},{10,9},{11,1... | collective-permute-start | bytes 786440 | tf_op jit(solution)/shard_map/while/body/eval_jaxpr/ppermute | solution.py:29
  419.2 10.8 %collective-permute-start.4 = (bf16[1,16,16,512]{3,2,1,0:T(8,128)(2,1)S(1)}, bf16[1,16,16,512]{3,2,1,0:T(8,128)(2,1)S(1)}, u32[]{:S(2)}, u32[]{:S(2)}) collective-permute-start(bf16[1,16,16,512]{3,2,1,0:T(8,128)(2,1)S(1)} %get-tuple-element.378), channel_id=1, source_target_pairs={{0,1},{1,2},{2,3},{3,4},{4,5},{5,6},{6,7},{7,8},{8,9},{9,10},{10,1... | collective-permute-start | bytes 786440 | tf_op jit(solution)/shard_map/while/body/eval_jaxpr/ppermute | solution.py:27
  421.2 13.3 %collective-permute-start.5 = (bf16[1,16,16,512]{3,2,1,0:T(8,128)(2,1)S(1)}, bf16[1,16,16,512]{3,2,1,0:T(8,128)(2,1)S(1)}, u32[]{:S(2)}, u32[]{:S(2)}) collective-permute-start(bf16[1,16,16,512]{3,2,1,0:T(8,128)(2,1)S(1)} %get-tuple-element.378), channel_id=1, source_target_pairs={{1,0},{2,1},{3,2},{4,3},{5,4},{6,5},{7,6},{8,7},{9,8},{10,9},{11,1... | collective-permute-start | bytes 786440 | tf_op jit(solution)/shard_map/while/body/eval_jaxpr/ppermute | solution.py:29
  476.5 10.7 %collective-permute-start.4 = (bf16[1,16,16,512]{3,2,1,0:T(8,128)(2,1)S(1)}, bf16[1,16,16,512]{3,2,1,0:T(8,128)(2,1)S(1)}, u32[]{:S(2)}, u32[]{:S(2)}) collective-permute-start(bf16[1,16,16,512]{3,2,1,0:T(8,128)(2,1)S(1)} %get-tuple-element.378), channel_id=1, source_target_pairs={{0,1},{1,2},{2,3},{3,4},{4,5},{5,6},{6,7},{7,8},{8,9},{9,10},{10,1... | collective-permute-start | bytes 786440 | tf_op jit(solution)/shard_map/while/body/eval_jaxpr/ppermute | solution.py:27
  491.1 18.7 %collective-permute-start = (bf16[1,16,16,512]{3,2,1,0:T(8,128)(2,1)}, bf16[1,16,16,512]{3,2,1,0:T(8,128)(2,1)S(1)}, u32[]{:S(2)}, u32[]{:S(2)}) collective-permute-start(bf16[1,16,16,512]{3,2,1,0:T(8,128)(2,1)} %get-tuple-element.343), channel_id=1, source_target_pairs={{0,32},{32,64},{64,96},{96,128},{128,160},{160,192},{192,224},{1,3... | collective-permute-start | bytes 786440 | tf_op jit(solution)/shard_map/while/body/eval_jaxpr/ppermute | solution.py:12
  510.8 11.3 %collective-permute-start.1 = (bf16[1,16,16,512]{3,2,1,0:T(8,128)(2,1)S(1)}, bf16[1,16,16,512]{3,2,1,0:T(8,128)(2,1)S(1)}, u32[]{:S(2)}, u32[]{:S(2)}) collective-permute-start(bf16[1,16,16,512]{3,2,1,0:T(8,128)(2,1)S(1)} %bitcast_select_fusion.2), channel_id=1, source_target_pairs={{0,32},{32,0},{64,96},{96,64},{128,160},{160,128},{192,224},{224,1... | collective-permute-start | bytes 786440 | tf_op jit(solution)/shard_map/while/body/eval_jaxpr/ppermute | solution.py:16
  538.7 10.8 %collective-permute-start.4 = (bf16[1,16,16,512]{3,2,1,0:T(8,128)(2,1)S(1)}, bf16[1,16,16,512]{3,2,1,0:T(8,128)(2,1)S(1)}, u32[]{:S(2)}, u32[]{:S(2)}) collective-permute-start(bf16[1,16,16,512]{3,2,1,0:T(8,128)(2,1)S(1)} %get-tuple-element.378), channel_id=1, source_target_pairs={{0,1},{1,2},{2,3},{3,4},{4,5},{5,6},{6,7},{7,8},{8,9},{9,10},{10,1... | collective-permute-start | bytes 786440 | tf_op jit(solution)/shard_map/while/body/eval_jaxpr/ppermute | solution.py:27
  540.6 13.0 %collective-permute-start.5 = (bf16[1,16,16,512]{3,2,1,0:T(8,128)(2,1)S(1)}, bf16[1,16,16,512]{3,2,1,0:T(8,128)(2,1)S(1)}, u32[]{:S(2)}, u32[]{:S(2)}) collective-permute-start(bf16[1,16,16,512]{3,2,1,0:T(8,128)(2,1)S(1)} %get-tuple-element.378), channel_id=1, source_target_pairs={{1,0},{2,1},{3,2},{4,3},{5,4},{6,5},{7,6},{8,7},{9,8},{10,9},{11,1... | collective-permute-start | bytes 786440 | tf_op jit(solution)/shard_map/while/body/eval_jaxpr/ppermute | solution.py:29
  562.9 21.5 %collective-permute-start.1 = (bf16[1,16,16,512]{3,2,1,0:T(8,128)(2,1)S(1)}, bf16[1,16,16,512]{3,2,1,0:T(8,128)(2,1)S(1)}, u32[]{:S(2)}, u32[]{:S(2)}) collective-permute-start(bf16[1,16,16,512]{3,2,1,0:T(8,128)(2,1)S(1)} %bitcast_select_fusion.2), channel_id=1, source_target_pairs={{0,32},{32,0},{64,96},{96,64},{128,160},{160,128},{192,224},{224,1... | collective-permute-start | bytes 786440 | tf_op jit(solution)/shard_map/while/body/eval_jaxpr/ppermute | solution.py:16
  601.8 10.8 %collective-permute-start.4 = (bf16[1,16,16,512]{3,2,1,0:T(8,128)(2,1)S(1)}, bf16[1,16,16,512]{3,2,1,0:T(8,128)(2,1)S(1)}, u32[]{:S(2)}, u32[]{:S(2)}) collective-permute-start(bf16[1,16,16,512]{3,2,1,0:T(8,128)(2,1)S(1)} %get-tuple-element.378), channel_id=1, source_target_pairs={{0,1},{1,2},{2,3},{3,4},{4,5},{5,6},{6,7},{7,8},{8,9},{9,10},{10,1... | collective-permute-start | bytes 786440 | tf_op jit(solution)/shard_map/while/body/eval_jaxpr/ppermute | solution.py:27
  603.8 12.2 %collective-permute-start.5 = (bf16[1,16,16,512]{3,2,1,0:T(8,128)(2,1)S(1)}, bf16[1,16,16,512]{3,2,1,0:T(8,128)(2,1)S(1)}, u32[]{:S(2)}, u32[]{:S(2)}) collective-permute-start(bf16[1,16,16,512]{3,2,1,0:T(8,128)(2,1)S(1)} %get-tuple-element.378), channel_id=1, source_target_pairs={{1,0},{2,1},{3,2},{4,3},{5,4},{6,5},{7,6},{8,7},{9,8},{10,9},{11,1... | collective-permute-start | bytes 786440 | tf_op jit(solution)/shard_map/while/body/eval_jaxpr/ppermute | solution.py:29
  637.9 16.8 %collective-permute-start.2 = (bf16[1,16,16,512]{3,2,1,0:T(8,128)(2,1)S(1)}, bf16[1,16,16,512]{3,2,1,0:T(8,128)(2,1)S(1)}, u32[]{:S(2)}, u32[]{:S(2)}) collective-permute-start(bf16[1,16,16,512]{3,2,1,0:T(8,128)(2,1)S(1)} %collective-permute-done.1), channel_id=1, source_target_pairs={{0,64},{32,96},{64,0},{96,32},{128,192},{160,224},{192,128},{224,1... | collective-permute-start | bytes 786440 | tf_op jit(solution)/shard_map/while/body/eval_jaxpr/ppermute | solution.py:16
  664.9 10.8 %collective-permute-start.4 = (bf16[1,16,16,512]{3,2,1,0:T(8,128)(2,1)S(1)}, bf16[1,16,16,512]{3,2,1,0:T(8,128)(2,1)S(1)}, u32[]{:S(2)}, u32[]{:S(2)}) collective-permute-start(bf16[1,16,16,512]{3,2,1,0:T(8,128)(2,1)S(1)} %get-tuple-element.378), channel_id=1, source_target_pairs={{0,1},{1,2},{2,3},{3,4},{4,5},{5,6},{6,7},{7,8},{8,9},{9,10},{10,1... | collective-permute-start | bytes 786440 | tf_op jit(solution)/shard_map/while/body/eval_jaxpr/ppermute | solution.py:27
  666.8 10.7 %collective-permute-start.5 = (bf16[1,16,16,512]{3,2,1,0:T(8,128)(2,1)S(1)}, bf16[1,16,16,512]{3,2,1,0:T(8,128)(2,1)S(1)}, u32[]{:S(2)}, u32[]{:S(2)}) collective-permute-start(bf16[1,16,16,512]{3,2,1,0:T(8,128)(2,1)S(1)} %get-tuple-element.378), channel_id=1, source_target_pairs={{1,0},{2,1},{3,2},{4,3},{5,4},{6,5},{7,6},{8,7},{9,8},{10,9},{11,1... | collective-permute-start | bytes 786440 | tf_op jit(solution)/shard_map/while/body/eval_jaxpr/ppermute | solution.py:29
  679.6 10.7 collective-permute-start
  699.2 17.3 %collective-permute-start.2 = (bf16[1,16,16,512]{3,2,1,0:T(8,128)(2,1)S(1)}, bf16[1,16,16,512]{3,2,1,0:T(8,128)(2,1)S(1)}, u32[]{:S(2)}, u32[]{:S(2)}) collective-permute-start(bf16[1,16,16,512]{3,2,1,0:T(8,128)(2,1)S(1)} %collective-permute-done.1), channel_id=1, source_target_pairs={{0,64},{32,96},{64,0},{96,32},{128,192},{160,224},{192,128},{224,1... | collective-permute-start | bytes 786440 | tf_op jit(solution)/shard_map/while/body/eval_jaxpr/ppermute | solution.py:16
  727.6 10.8 %collective-permute-start.4 = (bf16[1,16,16,512]{3,2,1,0:T(8,128)(2,1)S(1)}, bf16[1,16,16,512]{3,2,1,0:T(8,128)(2,1)S(1)}, u32[]{:S(2)}, u32[]{:S(2)}) collective-permute-start(bf16[1,16,16,512]{3,2,1,0:T(8,128)(2,1)S(1)} %get-tuple-element.378), channel_id=1, source_target_pairs={{0,1},{1,2},{2,3},{3,4},{4,5},{5,6},{6,7},{7,8},{8,9},{9,10},{10,1... | collective-permute-start | bytes 786440 | tf_op jit(solution)/shard_map/while/body/eval_jaxpr/ppermute | solution.py:27
  729.6 13.1 %collective-permute-start.5 = (bf16[1,16,16,512]{3,2,1,0:T(8,128)(2,1)S(1)}, bf16[1,16,16,512]{3,2,1,0:T(8,128)(2,1)S(1)}, u32[]{:S(2)}, u32[]{:S(2)}) collective-permute-start(bf16[1,16,16,512]{3,2,1,0:T(8,128)(2,1)S(1)} %get-tuple-element.378), channel_id=1, source_target_pairs={{1,0},{2,1},{3,2},{4,3},{5,4},{6,5},{7,6},{8,7},{9,8},{10,9},{11,1... | collective-permute-start | bytes 786440 | tf_op jit(solution)/shard_map/while/body/eval_jaxpr/ppermute | solution.py:29
  767.6 23.5 %collective-permute-start.3 = (bf16[1,16,16,512]{3,2,1,0:T(8,128)(2,1)S(1)}, bf16[1,16,16,512]{3,2,1,0:T(8,128)(2,1)S(1)}, u32[]{:S(2)}, u32[]{:S(2)}) collective-permute-start(bf16[1,16,16,512]{3,2,1,0:T(8,128)(2,1)S(1)} %collective-permute-done.2), channel_id=1, source_target_pairs={{0,128},{32,160},{64,192},{96,224},{128,0},{160,32},{192,64},{224,... | collective-permute-start | bytes 786440 | tf_op jit(solution)/shard_map/while/body/eval_jaxpr/ppermute | solution.py:16
  791.7 10.8 %collective-permute-start.4 = (bf16[1,16,16,512]{3,2,1,0:T(8,128)(2,1)S(1)}, bf16[1,16,16,512]{3,2,1,0:T(8,128)(2,1)S(1)}, u32[]{:S(2)}, u32[]{:S(2)}) collective-permute-start(bf16[1,16,16,512]{3,2,1,0:T(8,128)(2,1)S(1)} %get-tuple-element.378), channel_id=1, source_target_pairs={{0,1},{1,2},{2,3},{3,4},{4,5},{5,6},{6,7},{7,8},{8,9},{9,10},{10,1... | collective-permute-start | bytes 786440 | tf_op jit(solution)/shard_map/while/body/eval_jaxpr/ppermute | solution.py:27
  793.6 13.3 %collective-permute-start.5 = (bf16[1,16,16,512]{3,2,1,0:T(8,128)(2,1)S(1)}, bf16[1,16,16,512]{3,2,1,0:T(8,128)(2,1)S(1)}, u32[]{:S(2)}, u32[]{:S(2)}) collective-permute-start(bf16[1,16,16,512]{3,2,1,0:T(8,128)(2,1)S(1)} %get-tuple-element.378), channel_id=1, source_target_pairs={{1,0},{2,1},{3,2},{4,3},{5,4},{6,5},{7,6},{8,7},{9,8},{10,9},{11,1... | collective-permute-start | bytes 786440 | tf_op jit(solution)/shard_map/while/body/eval_jaxpr/ppermute | solution.py:29
  835.9 20.8 %collective-permute-start.3 = (bf16[1,16,16,512]{3,2,1,0:T(8,128)(2,1)S(1)}, bf16[1,16,16,512]{3,2,1,0:T(8,128)(2,1)S(1)}, u32[]{:S(2)}, u32[]{:S(2)}) collective-permute-start(bf16[1,16,16,512]{3,2,1,0:T(8,128)(2,1)S(1)} %collective-permute-done.2), channel_id=1, source_target_pairs={{0,128},{32,160},{64,192},{96,224},{128,0},{160,32},{192,64},{224,... | collective-permute-start | bytes 786440 | tf_op jit(solution)/shard_map/while/body/eval_jaxpr/ppermute | solution.py:16
  857.3 10.8 %collective-permute-start.4 = (bf16[1,16,16,512]{3,2,1,0:T(8,128)(2,1)S(1)}, bf16[1,16,16,512]{3,2,1,0:T(8,128)(2,1)S(1)}, u32[]{:S(2)}, u32[]{:S(2)}) collective-permute-start(bf16[1,16,16,512]{3,2,1,0:T(8,128)(2,1)S(1)} %get-tuple-element.378), channel_id=1, source_target_pairs={{0,1},{1,2},{2,3},{3,4},{4,5},{5,6},{6,7},{7,8},{8,9},{9,10},{10,1... | collective-permute-start | bytes 786440 | tf_op jit(solution)/shard_map/while/body/eval_jaxpr/ppermute | solution.py:27
  859.2 13.3 %collective-permute-start.5 = (bf16[1,16,16,512]{3,2,1,0:T(8,128)(2,1)S(1)}, bf16[1,16,16,512]{3,2,1,0:T(8,128)(2,1)S(1)}, u32[]{:S(2)}, u32[]{:S(2)}) collective-permute-start(bf16[1,16,16,512]{3,2,1,0:T(8,128)(2,1)S(1)} %get-tuple-element.378), channel_id=1, source_target_pairs={{1,0},{2,1},{3,2},{4,3},{5,4},{6,5},{7,6},{8,7},{9,8},{10,9},{11,1... | collective-permute-start | bytes 786440 | tf_op jit(solution)/shard_map/while/body/eval_jaxpr/ppermute | solution.py:29
  (50 other events, 349.6 us)
Sparse Core Ops, SparseCore 0:
  10.0 55.0 all-gather.9
  67.7 60.6 all-gather.5
  131.1 60.4 all-gather.7
  875.9 177.5 all-gather.11
